TPU v7x, 32 devices: a whole 2x2x4 slice. The times are simulated.
32 devices in a mesh: row: 4 (over z), col: 8 (over y, x, core).
Axes of the slice: x: 2, y: 2, z: 4, core: 2. Of those that a mesh axis runs over, the one named last changes fastest.
Arguments:
- diag_factor: float32 [512, 512], P('row', 'col'), as said below
- panel_factor: float32 [8192, 512], P('row', 'col'), may hold values from -0.0625 to 0.0625
- row_factor: float32 [512, 3072], P('row', 'col'), may hold values from -0.25 to 0.25
- trailing_factor: float32 [8192, 3072], P('row', 'col'), may hold values from -0.0625 to 0.0625
- panel_grad: float32 [8192, 512], P('row', 'col'), may hold values from -6 to 6
- diag_grad: float32 [512, 512], P('row', 'col'), may hold values from -6 to 6
- row_grad: float32 [512, 3072], P('row', 'col'), may hold values from -6 to 6
- trailing_grad: float32 [8192, 3072], P('row', 'col'), may hold values from -6 to 6
Outputs:
- panel_adjoint: float32 [8192, 512], P('row', 'col')
- trailing_out: float32 [8192, 3072], P('row', 'col')
- row_out: float32 [512, 3072], P('row', 'col')
- diag_out: float32 [512, 512], P('row', 'col')
Inputs may be any that keep to these rules, and one draw needn't show every extreme that they name: diag_factor is zero above its diagonal; its diagonal entries lie between 1 and 2.
All inputs are finite; a program needn't handle non-finite values.
Results may differ from a plain program's by a relative error of at most 0.00011.
Values sent between devices are 32-bit elements; how exact they have to be, the bound alone decides.
A program may use at most 64 MiB of HBM per device.

v0:
```python
import jax
import jax.numpy as jnp
from jax import lax
from jax.sharding import PartitionSpec as P


def on_device(
    diag_factor,
    panel_factor,
    row_factor,
    trailing_factor,
    panel_grad,
    diag_grad,
    row_grad,
    trailing_grad,
):
    high = lax.Precision.HIGHEST
    tile_rows = lax.all_gather(diag_factor, "row", axis=0, tiled=True)
    whole_diag = lax.all_gather(tile_rows, "col", axis=1, tiled=True)
    width = panel_grad.shape[1]
    start_col = lax.axis_index("col") * width
    full_grad = lax.all_gather(panel_grad, "col", axis=1, tiled=True)
    solved = jax.scipy.linalg.solve_triangular(whole_diag, full_grad.T, lower=True, trans=1).T
    panel_adjoint = lax.dynamic_slice_in_dim(solved, start_col, width, 1)
    trailing_out = trailing_grad - jnp.dot(
        solved,
        lax.all_gather(row_factor, "row", axis=0, tiled=True),
        precision=high,
        preferred_element_type=jnp.float32,
    )
    contract = (((0,), (0,)), ((), ()))
    row_term = lax.dot_general(
        solved, trailing_factor, contract, precision=high, preferred_element_type=jnp.float32
    )
    diag_term = lax.dot_general(
        solved, panel_factor, contract, precision=high, preferred_element_type=jnp.float32
    )
    row_sum, diag_sum = (
        lax.psum_scatter(row_term, "row", scatter_dimension=0, tiled=True),
        lax.psum_scatter(diag_term, "row", scatter_dimension=0, tiled=True),
    )
    row_out = row_grad - row_sum
    height = diag_grad.shape[0]
    global_rows = lax.axis_index("row") * height + jnp.arange(height)[:, None]
    global_cols = start_col + jnp.arange(width)[None, :]
    diag_out = jnp.where(global_rows >= global_cols, diag_grad - diag_sum, jnp.float32(0.0))
    return (panel_adjoint, trailing_out, row_out, diag_out)


def solution(mesh):
    placed = (
        P("row", "col"),
        P("row", "col"),
        P("row", "col"),
        P("row", "col"),
        P("row", "col"),
        P("row", "col"),
        P("row", "col"),
        P("row", "col"),
    )
    return jax.shard_map(
        on_device,
        mesh=mesh,
        in_specs=placed,
        out_specs=(P("row", "col"), P("row", "col"), P("row", "col"), P("row", "col")),
        check_vma=False,
    )
```

profile of v0, /device:TPU:0, one launch (start us, length us, event | category | flops | bytes accessed | tf_op | source)
XLA Modules:
  0.0 176.6 jit_solution(3847113311811466690)
XLA Ops:
  7.2 0.0 copy-start
  7.2 0.0 all-gather.3.cloned.1.call-start
  7.2 17.2 %all_gather.12 = f32[512,64]{0,1:T(8,128)} all-gather(f32[128,64]{0,1:T(8,128)} %param.8), channel_id=1, replica_groups=mesh['row'=4,'col'=8] {'row'}, dimensions={0}, use_global_device_ids=true | all-gather | bytes 163840 | tf_op jit(solution)/shard_map/all_gather | solution.py:18
  24.4 0.0 all-gather.3.cloned.1.call-update
  24.4 0.0 all-gather.5.cloned.1.call-start
  24.5 0.7 all-gather.5.cloned.1.call-update
  25.2 0.0 reduce-scatter.5.cloned.1.call-start
  25.3 22.8 %all-gather.3.cloned.1.call-done = f32[512,512]{0,1:T(8,128)} async-done(((f32[512,64]{0,1:T(8,128)}), f32[512,512]{0,1:T(8,128)}) %all-gather.3.cloned.1.call-update) | async-done | bytes 1048592 | tf_op jit(solution)/shard_map/all_gather | solution.py:19
  48.1 2.3 %fusion.14 = f32[512,512]{0,1:T(8,128)} fusion(f32[512,512]{0,1:T(8,128)} %all-gather.3.cloned.1.call-done), kind=kLoop, calls=%fused_computation.19 | loop fusion | flops 524288 | bytes 2097152 | tf_op jit(solution)/shard_map/jit(_solve_triangular)/triangular_solve | solution.py:23
  50.4 14.1 %while.1 = (s32[]{:T(128)}, f32[512,512]{0,1:T(8,128)}, s32[4,2]{0,1:T(2,128)S(1)}, f32[4,128,128]{2,1,0:T(8,128)}, s32[]{:T(128)}) while((s32[]{:T(128)}, f32[512,512]{0,1:T(8,128)}, s32[4,2]{0,1:T(2,128)S(1)}, f32[4,128,128]{2,1,0:T(8,128)}, s32[]{:T(128)}) %tuple.24), condition=%wide.while_cond, body=%wide.while_body.sunk | while | flops 2 | bytes 393329 | solution.py:23
  50.4 0.1 constant_dynamic-slice_fusion.2
  50.5 0.5 fusion.34
  51.0 2.2 %dynamic-slice.12 = f32[128,128]{0,1:T(8,128)S(1)} dynamic-slice(f32[512,512]{0,1:T(8,128)} %get-tuple-element.66, s32[]{:T(128)} %bitcast.30, s32[]{:T(128)} %bitcast.31), dynamic_slice_sizes={128,128} | dynamic-slice | bytes 131076 | tf_op jit(solution)/shard_map/jit(_solve_triangular)/triangular_solve
  53.2 0.1 copy.16
  53.3 0.6 bitcast_dynamic-update-slice_fusion.2
  53.9 0.1 constant_dynamic-slice_fusion.2
  54.0 0.5 fusion.34
  54.5 2.2 %dynamic-slice.12 = f32[128,128]{0,1:T(8,128)S(1)} dynamic-slice(f32[512,512]{0,1:T(8,128)} %get-tuple-element.66, s32[]{:T(128)} %bitcast.30, s32[]{:T(128)} %bitcast.31), dynamic_slice_sizes={128,128} | dynamic-slice | bytes 131076 | tf_op jit(solution)/shard_map/jit(_solve_triangular)/triangular_solve
  56.8 0.1 copy.16
  56.9 0.6 bitcast_dynamic-update-slice_fusion.2
  57.5 0.1 constant_dynamic-slice_fusion.2
  57.6 0.5 fusion.34
  58.1 2.2 %dynamic-slice.12 = f32[128,128]{0,1:T(8,128)S(1)} dynamic-slice(f32[512,512]{0,1:T(8,128)} %get-tuple-element.66, s32[]{:T(128)} %bitcast.30, s32[]{:T(128)} %bitcast.31), dynamic_slice_sizes={128,128} | dynamic-slice | bytes 131076 | tf_op jit(solution)/shard_map/jit(_solve_triangular)/triangular_solve
  60.3 0.1 copy.16
  60.4 0.6 bitcast_dynamic-update-slice_fusion.2
  61.0 0.1 constant_dynamic-slice_fusion.2
  61.1 0.5 fusion.34
  61.6 2.1 %dynamic-slice.12 = f32[128,128]{0,1:T(8,128)S(1)} dynamic-slice(f32[512,512]{0,1:T(8,128)} %get-tuple-element.66, s32[]{:T(128)} %bitcast.30, s32[]{:T(128)} %bitcast.31), dynamic_slice_sizes={128,128} | dynamic-slice | bytes 131076 | tf_op jit(solution)/shard_map/jit(_solve_triangular)/triangular_solve
  63.8 0.1 copy.16
  63.9 0.6 bitcast_dynamic-update-slice_fusion.2
  64.5 40.3 %custom-call.4 = f32[4,128,128]{1,2,0:T(8,128)S(1)} custom-call(f32[4,128,128]{2,1,0:T(8,128)} %get-tuple-element.11), custom_call_target="InvertDiagBlocksLowerTriangular" | custom-call | tf_op jit(solution)/shard_map/jit(_solve_triangular)/triangular_solve | solution.py:23
  104.8 0.0 all-gather.5.cloned.1.call-done
  104.8 0.0 copy-start.9
  104.9 2.4 %fusion.12 = f32[128,2048]{1,0:T(8,128)S(1)} fusion(f32[512,2048]{1,0:T(8,128)} %bitcast.32, f32[4,128,128]{1,2,0:T(8,128)S(1)} %custom-call.4), kind=kOutput, calls=%fused_computation.16 | convolution fusion | flops 402653184 | bytes 2162688 | tf_op jit(solution)/shard_map/jit(_solve_triangular)/triangular_solve | solution.py:23
  107.2 0.0 copy-start.1
  107.2 2.7 %convolution_subtract_fusion.2 = f32[128,2048]{1,0:T(8,128)S(1)} fusion(f32[128,2048]{1,0:T(8,128)S(1)} %fusion.12, f32[512,2048]{1,0:T(8,128)} %bitcast.33, f32[512,512]{0,1:T(8,128)} %get-tuple-element.75), kind=kOutput, calls=%fused_computation.12 | convolution fusion | flops 402915328 | bytes 3211264 | tf_op jit(solution)/shard_map/jit(_solve_triangular)/triangular_solve | solution.py:23
  109.9 1.0 fusion.18
  110.9 0.0 copy-done.9
  110.9 0.0 copy-start.3
  110.9 2.3 %convolution_subtract_fusion.1 = f32[128,2048]{1,0:T(8,128)S(1)} fusion(f32[128,2048]{1,0:T(8,128)S(1)} %fusion.12, f32[128,2048]{1,0:T(8,128)S(1)} %fusion.18, f32[512,2048]{1,0:T(8,128)S(1)} %bitcast.34, f32[512,512]{0,1:T(8,128)} %get-tuple-element.75), kind=kOutput, calls=%fused_computation.11 | convolution fusion | flops 806092800 | bytes 4325376 | tf_op jit(solution)/shard_map/jit(_solve_triangular)/triangular_solve | solution.py:23
  113.3 1.0 fusion.19
  114.3 0.0 copy-start.5
  114.3 0.0 copy-start.14
  114.3 3.3 %fusion.6 = f32[128,2048]{1,0:T(8,128)S(1)} fusion(f32[128,2048]{1,0:T(8,128)S(1)} %fusion.12, f32[128,2048]{1,0:T(8,128)S(1)} %fusion.18, f32[128,2048]{1,0:T(8,128)S(1)} %fusion.19, f32[512,2048]{1,0:T(8,128)S(1)} %bitcast.35, f32[512,512]{0,1:T(8,128)} %get-tuple-element.75), kind=kOutput, calls=%fused_computation.10 | convolution fusion | flops 1209794560 | bytes 5439488 | tf_op jit(solution)/shard_map/jit(_solve_triangular)/triangular_solve | solution.py:23
  117.6 1.0 fusion.20
  118.6 0.0 copy-done.1
  118.7 0.0 copy-done.3
  118.7 0.0 copy-done.5
  118.7 0.0 copy-start.7
  118.7 1.0 copy-done.7
  119.6 4.8 %fusion.23 = f32[512,64]{0,1:T(8,128)} fusion(f32[2048,64]{0,1:T(8,128)S(1)} %copy-done.14, f32[128,2048]{1,0:T(8,128)S(1)} %fusion.12, f32[128,2048]{1,0:T(8,128)S(1)} %fusion.18, f32[128,2048]{1,0:T(8,128)S(1)} %fusion.19, f32[128,2048]{1,0:T(8,128)S(1)} %fusion.20), kind=kOutput, calls=%fused_computation.37 | convolution fusion | flops 808452096 | bytes 4849664 | tf_op jit(solution)/shard_map/dot_general | solution.py:35
  124.5 0.0 reduce-scatter.5.cloned.1.call-update
  124.5 0.0 copy-start.12
  124.5 0.0 reduce-scatter.3.cloned.1.call-start
  124.6 9.5 %fusion.24 = f32[512,384]{1,0:T(8,128)} fusion(f32[2048,384]{1,0:T(8,128)S(1)} %copy-done, f32[128,2048]{1,0:T(8,128)} %copy-done.1, f32[128,2048]{1,0:T(8,128)} %copy-done.3, f32[128,2048]{1,0:T(8,128)} %copy-done.5, f32[128,2048]{1,0:T(8,128)} %copy-done.7), kind=kOutput, calls=%fused_computation.38 | convolution fusion | flops 4834983936 | bytes 8126464 | tf_op jit(solution)/shard_map/dot_general | solution.py:32
  134.1 0.0 reduce-scatter.3.cloned.1.call-update
  134.2 19.7 %all_gather.15 = f32[512,384]{1,0:T(8,128)S(1)} all-gather(f32[128,384]{1,0:T(8,128)S(1)} %copy-done.12), channel_id=1, replica_groups=mesh['row'=4,'col'=8] {'row'}, dimensions={0}, use_global_device_ids=true | all-gather | bytes 983040 | tf_op jit(solution)/shard_map/all_gather | solution.py:27
  153.9 0.0 copy-start.10
  153.9 2.8 %pad_maximum_fusion = f32[512,2048]{1,0:T(8,128)S(1)} fusion(f32[128,2048]{1,0:T(8,128)} %copy-done.1, f32[128,2048]{1,0:T(8,128)} %copy-done.3, f32[128,2048]{1,0:T(8,128)} %copy-done.5, f32[128,2048]{1,0:T(8,128)} %copy-done.7), kind=kLoop, calls=%fused_computation.2 | loop fusion | flops 3145728 | bytes 8388608 | tf_op jit(solution)/shard_map/jit(_solve_triangular)/triangular_solve | solution.py:23
  156.7 0.8 dynamic-slice_bitcast_fusion
  157.6 1.0 copy-done.10
  158.6 8.4 %convolution_subtract_fusion = f32[2048,384]{1,0:T(8,128)} fusion(f32[2048,384]{1,0:T(8,128)S(1)} %copy-done.10, f32[512,384]{1,0:T(8,128)S(1)} %all_gather.15, f32[128,2048]{1,0:T(8,128)S(1)} %copy-done.2, f32[128,2048]{1,0:T(8,128)S(1)} %copy-done.4, f32[128,2048]{1,0:T(8,128)S(1)} %copy-done.6, f32[128,2048]{1,0:T(8,128)S(1)} %copy-done.8), kind=kOutput, calls=%fused_computation.9 | convolution fusion | flops 4835770368 | bytes 11272192 | tf_op jit(solution)/shard_map/dot_general | solution.py:25
  167.0 1.4 subtract_select_fusion
  168.4 1.6 sub.10
  (22 shorter events, 0.0 us)
Async XLA Ops:
  7.2 117.4 %copy-start = (f32[2048,384]{1,0:T(8,128)S(1)}, f32[2048,384]{1,0:T(8,128)}, u32[]{:S(2)}) copy-start(f32[2048,384]{1,0:T(8,128)} %param.11) | copy-start | bytes 9437188
  7.2 40.9 %all-gather.3.cloned.1.call-start = ((), (), s32[]{:S(2)}) async-start(), calls=%async_computation.2 | async-start | bytes 1179648 | tf_op jit(solution)/shard_map/all_gather | solution.py:19
  24.4 80.4 %all-gather.5.cloned.1.call-start = ((), (), s32[]{:S(2)}) async-start(), calls=%async_computation.3 | async-start | bytes 4718592 | tf_op jit(solution)/shard_map/all_gather | solution.py:22
  25.2 141.8 %reduce-scatter.5.cloned.1.call-start = ((), (), s32[]{:S(2)}) async-start(), calls=%async_computation.5 | async-start | bytes 163840 | tf_op jit(solution)/shard_map/reduce_scatter | solution.py:40
  104.8 6.1 %copy-start.9 = (f32[2048,512]{0,1:T(8,128)S(1)}, f32[2048,512]{0,1:T(8,128)}, u32[]{:S(2)}) copy-start(f32[2048,512]{0,1:T(8,128)} %all-gather.5.cloned.1.call-done) | copy-start | bytes 12582916
  107.2 11.4 %copy-start.1 = (f32[128,2048]{1,0:T(8,128)}, f32[128,2048]{1,0:T(8,128)S(1)}, u32[]{:S(2)}) copy-start(f32[128,2048]{1,0:T(8,128)S(1)} %fusion.12) | copy-start | bytes 3145732
  110.9 7.7 %copy-start.3 = (f32[128,2048]{1,0:T(8,128)}, f32[128,2048]{1,0:T(8,128)S(1)}, u32[]{:S(2)}) copy-start(f32[128,2048]{1,0:T(8,128)S(1)} %fusion.18) | copy-start | bytes 3145732
  114.3 4.3 %copy-start.5 = (f32[128,2048]{1,0:T(8,128)}, f32[128,2048]{1,0:T(8,128)S(1)}, u32[]{:S(2)}) copy-start(f32[128,2048]{1,0:T(8,128)S(1)} %fusion.19) | copy-start | bytes 3145732
  114.3 5.3 %copy-start.14 = (f32[2048,64]{0,1:T(8,128)S(1)}, f32[2048,64]{0,1:T(8,128)}, u32[]{:S(2)}) copy-start(f32[2048,64]{0,1:T(8,128)} %param.9) | copy-start | bytes 1572868
  118.7 1.0 copy-start.7
  124.5 9.7 %copy-start.12 = (f32[128,384]{1,0:T(8,128)S(1)}, f32[128,384]{1,0:T(8,128)}, u32[]{:S(2)}) copy-start(f32[128,384]{1,0:T(8,128)} %param.10) | copy-start | bytes 589828
  124.5 43.9 %reduce-scatter.3.cloned.1.call-start = ((), (), s32[]{:S(2)}) async-start(), calls=%async_computation.4 | async-start | bytes 983040 | tf_op jit(solution)/shard_map/reduce_scatter | solution.py:39
  153.9 3.7 %copy-start.2 = (f32[128,2048]{1,0:T(8,128)S(1)}, f32[128,2048]{1,0:T(8,128)}, u32[]{:S(2)}) copy-start(f32[128,2048]{1,0:T(8,128)} %copy-done.1) | copy-start | bytes 3145732
  153.9 3.7 %copy-start.4 = (f32[128,2048]{1,0:T(8,128)S(1)}, f32[128,2048]{1,0:T(8,128)}, u32[]{:S(2)}) copy-start(f32[128,2048]{1,0:T(8,128)} %copy-done.3) | copy-start | bytes 3145732
  153.9 3.7 %copy-start.6 = (f32[128,2048]{1,0:T(8,128)S(1)}, f32[128,2048]{1,0:T(8,128)}, u32[]{:S(2)}) copy-start(f32[128,2048]{1,0:T(8,128)} %copy-done.5) | copy-start | bytes 3145732
  153.9 3.7 %copy-start.8 = (f32[128,2048]{1,0:T(8,128)S(1)}, f32[128,2048]{1,0:T(8,128)}, u32[]{:S(2)}) copy-start(f32[128,2048]{1,0:T(8,128)} %copy-done.7) | copy-start | bytes 3145732
  153.9 4.7 %copy-start.10 = (f32[2048,384]{1,0:T(8,128)S(1)}, f32[2048,384]{1,0:T(8,128)}, u32[]{:S(2)}) copy-start(f32[2048,384]{1,0:T(8,128)} %param.15) | copy-start | bytes 9437188
  158.6 8.4 %copy-start.13 = (f32[128,64]{0,1:T(8,128)S(1)}, f32[128,64]{0,1:T(8,128)}, u32[]{:S(2)}) copy-start(f32[128,64]{0,1:T(8,128)} %param.13) | copy-start | bytes 98308
  158.6 9.8 %copy-start.11 = (f32[128,384]{1,0:T(8,128)S(1)}, f32[128,384]{1,0:T(8,128)}, u32[]{:S(2)}) copy-start(f32[128,384]{1,0:T(8,128)} %param.14) | copy-start | bytes 589828
Sparse Core Ops, SparseCore 0:
  24.5 23.4 all-gather.2
  50.0 37.0 all-gather.4
  124.6 19.6 reduce-scatter.4
  146.5 21.3 reduce-scatter.2
where the time goes:
time: 177 us
  other arithmetic  48.5 us (27%)
  blocking collectives  36.9 us (21%)
  matrix products  36.5 us (21%)
  waiting for transfers between devices  23.6 us (13%)
  local copies, waits for them, and re-layouts  16.9 us (10%)
  between operations  14 us (8%)
    another operation x4, other arithmetic, on_device(): jax.scipy.linalg.solve_triangular(whole_diag, full_grad.T, lower=True, tr...  45.4 us
    all_gather x1, waiting for transfers between devices, on_device(): whole_diag = lax.all_gather(tile_rows, 'col', axis=1, tiled=True)  22.8 us
    all_gather x1, blocking collectives, on_device(): lax.all_gather(row_factor, 'row', axis=0, tiled=True)  19.7 us
    all_gather x1, blocking collectives, on_device(): tile_rows = lax.all_gather(diag_factor, 'row', axis=0, tiled=True)  17.2 us
    another operation x20, local copies, waits for them, and re-layouts  14.1 us
    another operation x7, matrix products, on_device(): jax.scipy.linalg.solve_triangular(whole_diag, full_grad.T, lower=True, tr...  13.7 us
    dot_general x1, matrix products, on_device(): lax.dot_general(solved, trailing_factor, contract, precision=high, prefer...  9.55 us
    dot_general x1, matrix products, on_device(): jnp.dot(solved, lax.all_gather(row_factor, 'row', axis=0, tiled=True), pr...  8.39 us
  transfers between devices with their start and end apart: 4, of which 1 were waited for; matrix products, arithmetic and copies ran while one was open for 45% of the time, Pallas kernels for 0%

commit v1 on v0

--- a/solution.py
+++ b/solution.py
@@ -16,10 +16,13 @@
 ):
     high = lax.Precision.HIGHEST
     tile_rows = lax.all_gather(diag_factor, "row", axis=0, tiled=True)
-    whole_diag = lax.all_gather(tile_rows, "col", axis=1, tiled=True)
     width = panel_grad.shape[1]
     start_col = lax.axis_index("col") * width
-    full_grad = lax.all_gather(panel_grad, "col", axis=1, tiled=True)
+    whole_diag, full_grad = jnp.split(
+        lax.all_gather(jnp.concatenate([tile_rows, panel_grad], axis=0), "col", axis=1, tiled=True),
+        [tile_rows.shape[0]],
+        axis=0,
+    )
     solved = jax.scipy.linalg.solve_triangular(whole_diag, full_grad.T, lower=True, trans=1).T
     panel_adjoint = lax.dynamic_slice_in_dim(solved, start_col, width, 1)
     trailing_out = trailing_grad - jnp.dot(

time: 177 us -> 197 us (1.11)
  waiting for transfers between devices: 23.6 us -> 42.5 us
  local copies, waits for them, and re-layouts: 16.9 us -> 20.2 us
  matrix products: 36.5 us -> 34.4 us
    all_gather x2 -> x1, waiting for transfers between devices: 22.8 us -> 42.4 us  [on_device(): lax.all_gather(jnp.concatenate([tile_rows, panel_grad], axis=0), 'col', a...]
    transpose x0 -> x1, local copies, waits for them, and re-layouts: none -> 2.46 us  [on_device(): solved = jax.scipy.linalg.solve_triangular(whole_diag, full_grad.T, lower...]
    another operation x7, matrix products: 13.7 us -> 11.5 us  [on_device(): jax.scipy.linalg.solve_triangular(whole_diag, full_grad.T, lower=True, tr...]
  transfers between devices with their start and end apart: 4 -> 3, of which waited for: 1 -> 1; matrix products, arithmetic and copies ran while one was open for 45% -> 12% of each run, Pallas kernels for 0% -> 0%
where the time goes in v1:
time: 197 us
  other arithmetic  50.4 us (26%)
  waiting for transfers between devices  42.5 us (22%)
  blocking collectives  35.2 us (18%)
  matrix products  34.4 us (17%)
  local copies, waits for them, and re-layouts  20.2 us (10%)
  between operations  14 us (7%)
    another operation x4, other arithmetic, on_device(): jax.scipy.linalg.solve_triangular(whole_diag, full_grad.T, lower=True, tr...  45.4 us
    all_gather x1, waiting for transfers between devices, on_device(): lax.all_gather(jnp.concatenate([tile_rows, panel_grad], axis=0), 'col', a...  42.4 us
    all_gather x1, blocking collectives, on_device(): lax.all_gather(row_factor, 'row', axis=0, tiled=True)  19.7 us
    all_gather x1, blocking collectives, on_device(): tile_rows = lax.all_gather(diag_factor, 'row', axis=0, tiled=True)  15.4 us
    another operation x20, local copies, waits for them, and re-layouts  14.9 us
    another operation x7, matrix products, on_device(): jax.scipy.linalg.solve_triangular(whole_diag, full_grad.T, lower=True, tr...  11.5 us
    dot_general x1, matrix products, on_device(): lax.dot_general(solved, trailing_factor, contract, precision=high, prefer...  9.57 us
    dot_general x1, matrix products, on_device(): jnp.dot(solved, lax.all_gather(row_factor, 'row', axis=0, tiled=True), pr...  8.39 us
  transfers between devices with their start and end apart: 3, of which 1 were waited for; matrix products, arithmetic and copies ran while one was open for 12% of the time, Pallas kernels for 0%

profile of v1, /device:TPU:0, one launch (start us, length us, event | category | flops | bytes accessed | tf_op | source)
XLA Modules:
  0.0 196.7 jit_solution(9679805122472735933)
XLA Ops:
  7.2 0.0 copy-start
  7.2 0.0 all-gather.2.cloned.1.call-start
  7.2 15.4 %all_gather.9 = f32[512,64]{0,1:T(8,128)S(1)} all-gather(f32[128,64]{0,1:T(8,128)} %param.8), channel_id=1, replica_groups=mesh['row'=4,'col'=8] {'row'}, dimensions={0}, use_global_device_ids=true | all-gather | bytes 163840 | tf_op jit(solution)/shard_map/all_gather | solution.py:18
  22.7 1.9 pad_maximum_fusion.1
  24.6 0.0 all-gather.2.cloned.1.call-update
  24.6 0.0 reduce-scatter.5.cloned.1.call-start
  24.7 42.4 %all-gather.2.cloned.1.call-done = f32[2560,512]{0,1:T(8,128)} async-done(((f32[2560,64]{0,1:T(8,128)}), f32[2560,512]{0,1:T(8,128)}) %all-gather.2.cloned.1.call-update) | async-done | bytes 5242896 | tf_op jit(solution)/shard_map/all_gather | solution.py:22
  67.1 2.3 %slice_select_fusion = f32[512,512]{0,1:T(8,128)} fusion(f32[2560,512]{0,1:T(8,128)} %all-gather.2.cloned.1.call-done), kind=kLoop, calls=%fused_computation.19 | loop fusion | flops 524288 | bytes 2097152 | tf_op jit(solution)/shard_map/jit(_solve_triangular)/triangular_solve | solution.py:26
  69.4 14.9 %while.1 = (s32[]{:T(128)}, f32[512,512]{0,1:T(8,128)}, s32[4,2]{0,1:T(2,128)S(1)}, f32[4,128,128]{2,1,0:T(8,128)}, s32[]{:T(128)}) while((s32[]{:T(128)}, f32[512,512]{0,1:T(8,128)}, s32[4,2]{0,1:T(2,128)S(1)}, f32[4,128,128]{2,1,0:T(8,128)}, s32[]{:T(128)}) %tuple.24), condition=%wide.while_cond, body=%wide.while_body.sunk | while | flops 2 | bytes 393329 | solution.py:26
  69.4 0.1 constant_dynamic-slice_fusion.2
  69.5 0.6 fusion.33
  70.1 2.3 %dynamic-slice.12 = f32[128,128]{0,1:T(8,128)S(1)} dynamic-slice(f32[512,512]{0,1:T(8,128)} %get-tuple-element.66, s32[]{:T(128)} %bitcast.31, s32[]{:T(128)} %bitcast.32), dynamic_slice_sizes={128,128} | dynamic-slice | bytes 131076 | tf_op jit(solution)/shard_map/jit(_solve_triangular)/triangular_solve
  72.4 0.1 copy.17
  72.5 0.6 bitcast_dynamic-update-slice_fusion.2
  73.2 0.1 constant_dynamic-slice_fusion.2
  73.2 0.6 fusion.33
  73.8 2.3 %dynamic-slice.12 = f32[128,128]{0,1:T(8,128)S(1)} dynamic-slice(f32[512,512]{0,1:T(8,128)} %get-tuple-element.66, s32[]{:T(128)} %bitcast.31, s32[]{:T(128)} %bitcast.32), dynamic_slice_sizes={128,128} | dynamic-slice | bytes 131076 | tf_op jit(solution)/shard_map/jit(_solve_triangular)/triangular_solve
  76.2 0.1 copy.17
  76.3 0.6 bitcast_dynamic-update-slice_fusion.2
  76.9 0.1 constant_dynamic-slice_fusion.2
  77.0 0.6 fusion.33
  77.6 2.3 %dynamic-slice.12 = f32[128,128]{0,1:T(8,128)S(1)} dynamic-slice(f32[512,512]{0,1:T(8,128)} %get-tuple-element.66, s32[]{:T(128)} %bitcast.31, s32[]{:T(128)} %bitcast.32), dynamic_slice_sizes={128,128} | dynamic-slice | bytes 131076 | tf_op jit(solution)/shard_map/jit(_solve_triangular)/triangular_solve
  79.9 0.1 copy.17
  80.0 0.6 bitcast_dynamic-update-slice_fusion.2
  80.7 0.1 constant_dynamic-slice_fusion.2
  80.7 0.6 fusion.33
  81.3 2.3 %dynamic-slice.12 = f32[128,128]{0,1:T(8,128)S(1)} dynamic-slice(f32[512,512]{0,1:T(8,128)} %get-tuple-element.66, s32[]{:T(128)} %bitcast.31, s32[]{:T(128)} %bitcast.32), dynamic_slice_sizes={128,128} | dynamic-slice | bytes 131076 | tf_op jit(solution)/shard_map/jit(_solve_triangular)/triangular_solve
  83.6 0.1 copy.17
  83.7 0.6 bitcast_dynamic-update-slice_fusion.2
  84.3 40.3 %custom-call.4 = f32[4,128,128]{1,2,0:T(8,128)S(1)} custom-call(f32[4,128,128]{2,1,0:T(8,128)} %get-tuple-element.11), custom_call_target="InvertDiagBlocksLowerTriangular" | custom-call | tf_op jit(solution)/shard_map/jit(_solve_triangular)/triangular_solve | solution.py:26
  124.6 2.5 %slice_bitcast_fusion = f32[512,2048]{1,0:T(8,128)S(1)} fusion(f32[2560,512]{0,1:T(8,128)} %all-gather.2.cloned.1.call-done), kind=kLoop, calls=%fused_computation.2 | loop fusion | bytes 8388608 | tf_op jit(solution)/shard_map/transpose | solution.py:26
  127.1 1.0 fusion.12
  128.1 0.0 copy-start.1
  128.1 1.9 convolution_subtract_fusion.2
  130.1 1.0 fusion.17
  131.1 0.0 copy-start.3
  131.1 2.3 %convolution_subtract_fusion.1 = f32[128,2048]{1,0:T(8,128)S(1)} fusion(f32[128,2048]{1,0:T(8,128)S(1)} %fusion.12, f32[128,2048]{1,0:T(8,128)S(1)} %fusion.17, f32[512,2048]{1,0:T(8,128)S(1)} %slice_bitcast_fusion, f32[512,512]{0,1:T(8,128)} %get-tuple-element.74), kind=kOutput, calls=%fused_computation.12 | convolution fusion | flops 806092800 | bytes 4325376 | tf_op jit(solution)/shard_map/jit(_solve_triangular)/triangular_solve | solution.py:26
  133.4 1.0 fusion.18
  134.4 0.0 copy-start.5
  134.4 0.0 copy-start.13
  134.4 3.3 %fusion.6 = f32[128,2048]{1,0:T(8,128)S(1)} fusion(f32[128,2048]{1,0:T(8,128)S(1)} %fusion.12, f32[128,2048]{1,0:T(8,128)S(1)} %fusion.17, f32[128,2048]{1,0:T(8,128)S(1)} %fusion.18, f32[512,2048]{1,0:T(8,128)S(1)} %slice_bitcast_fusion, f32[512,512]{0,1:T(8,128)} %get-tuple-element.74), kind=kOutput, calls=%fused_computation.11 | convolution fusion | flops 1209794560 | bytes 5439488 | tf_op jit(solution)/shard_map/jit(_solve_triangular)/triangular_solve | solution.py:26
  137.7 1.0 fusion.19
  138.7 0.0 copy-done.1
  138.8 0.0 copy-done.3
  138.8 0.0 copy-done.5
  138.8 0.0 copy-start.7
  138.8 1.0 copy-done.7
  139.7 0.0 copy-done.13
  139.7 4.9 %fusion.22 = f32[512,64]{0,1:T(8,128)} fusion(f32[2048,64]{0,1:T(8,128)S(1)} %copy-done.13, f32[128,2048]{1,0:T(8,128)S(1)} %fusion.12, f32[128,2048]{1,0:T(8,128)S(1)} %fusion.17, f32[128,2048]{1,0:T(8,128)S(1)} %fusion.18, f32[128,2048]{1,0:T(8,128)S(1)} %fusion.19), kind=kOutput, calls=%fused_computation.39 | convolution fusion | flops 808452096 | bytes 4849664 | tf_op jit(solution)/shard_map/dot_general | solution.py:38
  144.6 0.0 reduce-scatter.5.cloned.1.call-update
  144.6 0.0 copy-start.11
  144.7 0.0 reduce-scatter.3.cloned.1.call-start
  144.7 9.6 %fusion.23 = f32[512,384]{1,0:T(8,128)} fusion(f32[2048,384]{1,0:T(8,128)S(1)} %copy-done, f32[128,2048]{1,0:T(8,128)} %copy-done.1, f32[128,2048]{1,0:T(8,128)} %copy-done.3, f32[128,2048]{1,0:T(8,128)} %copy-done.5, f32[128,2048]{1,0:T(8,128)} %copy-done.7), kind=kOutput, calls=%fused_computation.40 | convolution fusion | flops 4834983936 | bytes 8126464 | tf_op jit(solution)/shard_map/dot_general | solution.py:35
  154.3 0.0 reduce-scatter.3.cloned.1.call-update
  154.3 19.7 %all_gather.11 = f32[512,384]{1,0:T(8,128)S(1)} all-gather(f32[128,384]{1,0:T(8,128)S(1)} %copy-done.11), channel_id=1, replica_groups=mesh['row'=4,'col'=8] {'row'}, dimensions={0}, use_global_device_ids=true | all-gather | bytes 983040 | tf_op jit(solution)/shard_map/all_gather | solution.py:30
  174.1 0.0 copy-start.9
  174.1 2.8 %pad_maximum_fusion = f32[512,2048]{1,0:T(8,128)S(1)} fusion(f32[128,2048]{1,0:T(8,128)} %copy-done.1, f32[128,2048]{1,0:T(8,128)} %copy-done.3, f32[128,2048]{1,0:T(8,128)} %copy-done.5, f32[128,2048]{1,0:T(8,128)} %copy-done.7), kind=kLoop, calls=%fused_computation.3 | loop fusion | flops 3145728 | bytes 8388608 | tf_op jit(solution)/shard_map/jit(_solve_triangular)/triangular_solve | solution.py:26
  176.9 0.8 dynamic-slice_bitcast_fusion
  177.8 0.0 copy-done.8
  177.8 1.0 copy-done.9
  178.7 8.4 %convolution_subtract_fusion = f32[2048,384]{1,0:T(8,128)} fusion(f32[2048,384]{1,0:T(8,128)S(1)} %copy-done.9, f32[512,384]{1,0:T(8,128)S(1)} %all_gather.11, f32[128,2048]{1,0:T(8,128)S(1)} %copy-done.2, f32[128,2048]{1,0:T(8,128)S(1)} %copy-done.4, f32[128,2048]{1,0:T(8,128)S(1)} %copy-done.6, f32[128,2048]{1,0:T(8,128)S(1)} %copy-done.8), kind=kOutput, calls=%fused_computation.10 | convolution fusion | flops 4835770368 | bytes 11272192 | tf_op jit(solution)/shard_map/dot_general | solution.py:28
  187.1 1.4 subtract_select_fusion
  188.6 0.0 copy-done.10
  188.6 1.6 sub.10
  (19 shorter events, 0.0 us)
Async XLA Ops:
  7.2 137.5 %copy-start = (f32[2048,384]{1,0:T(8,128)S(1)}, f32[2048,384]{1,0:T(8,128)}, u32[]{:S(2)}) copy-start(f32[2048,384]{1,0:T(8,128)} %param.11) | copy-start | bytes 9437188
  7.2 59.9 %all-gather.2.cloned.1.call-start = ((), (), s32[]{:S(2)}) async-start(), calls=%async_computation.2 | async-start | bytes 5898240 | tf_op jit(solution)/shard_map/all_gather | solution.py:22
  24.6 162.5 %reduce-scatter.5.cloned.1.call-start = ((), (), s32[]{:S(2)}) async-start(), calls=%async_computation.4 | async-start | bytes 163840 | tf_op jit(solution)/shard_map/reduce_scatter | solution.py:43
  128.1 10.6 %copy-start.1 = (f32[128,2048]{1,0:T(8,128)}, f32[128,2048]{1,0:T(8,128)S(1)}, u32[]{:S(2)}) copy-start(f32[128,2048]{1,0:T(8,128)S(1)} %fusion.12) | copy-start | bytes 3145732
  131.1 7.7 %copy-start.3 = (f32[128,2048]{1,0:T(8,128)}, f32[128,2048]{1,0:T(8,128)S(1)}, u32[]{:S(2)}) copy-start(f32[128,2048]{1,0:T(8,128)S(1)} %fusion.17) | copy-start | bytes 3145732
  134.4 4.3 %copy-start.5 = (f32[128,2048]{1,0:T(8,128)}, f32[128,2048]{1,0:T(8,128)S(1)}, u32[]{:S(2)}) copy-start(f32[128,2048]{1,0:T(8,128)S(1)} %fusion.18) | copy-start | bytes 3145732
  134.4 5.3 %copy-start.13 = (f32[2048,64]{0,1:T(8,128)S(1)}, f32[2048,64]{0,1:T(8,128)}, u32[]{:S(2)}) copy-start(f32[2048,64]{0,1:T(8,128)} %param.9) | copy-start | bytes 1572868
  138.8 1.0 copy-start.7
  144.6 9.7 %copy-start.11 = (f32[128,384]{1,0:T(8,128)S(1)}, f32[128,384]{1,0:T(8,128)}, u32[]{:S(2)}) copy-start(f32[128,384]{1,0:T(8,128)} %param.10) | copy-start | bytes 589828
  144.7 43.9 %reduce-scatter.3.cloned.1.call-start = ((), (), s32[]{:S(2)}) async-start(), calls=%async_computation.3 | async-start | bytes 983040 | tf_op jit(solution)/shard_map/reduce_scatter | solution.py:42
  174.1 3.7 %copy-start.2 = (f32[128,2048]{1,0:T(8,128)S(1)}, f32[128,2048]{1,0:T(8,128)}, u32[]{:S(2)}) copy-start(f32[128,2048]{1,0:T(8,128)} %copy-done.1) | copy-start | bytes 3145732
  174.1 3.7 %copy-start.4 = (f32[128,2048]{1,0:T(8,128)S(1)}, f32[128,2048]{1,0:T(8,128)}, u32[]{:S(2)}) copy-start(f32[128,2048]{1,0:T(8,128)} %copy-done.3) | copy-start | bytes 3145732
  174.1 3.7 %copy-start.6 = (f32[128,2048]{1,0:T(8,128)S(1)}, f32[128,2048]{1,0:T(8,128)}, u32[]{:S(2)}) copy-start(f32[128,2048]{1,0:T(8,128)} %copy-done.5) | copy-start | bytes 3145732
  174.1 3.7 %copy-start.8 = (f32[128,2048]{1,0:T(8,128)S(1)}, f32[128,2048]{1,0:T(8,128)}, u32[]{:S(2)}) copy-start(f32[128,2048]{1,0:T(8,128)} %copy-done.7) | copy-start | bytes 3145732
  174.1 4.7 %copy-start.9 = (f32[2048,384]{1,0:T(8,128)S(1)}, f32[2048,384]{1,0:T(8,128)}, u32[]{:S(2)}) copy-start(f32[2048,384]{1,0:T(8,128)} %param.15) | copy-start | bytes 9437188
  178.7 8.4 %copy-start.12 = (f32[128,64]{0,1:T(8,128)S(1)}, f32[128,64]{0,1:T(8,128)}, u32[]{:S(2)}) copy-start(f32[128,64]{0,1:T(8,128)} %param.13) | copy-start | bytes 98308
  178.7 9.8 %copy-start.10 = (f32[128,384]{1,0:T(8,128)S(1)}, f32[128,384]{1,0:T(8,128)}, u32[]{:S(2)}) copy-start(f32[128,384]{1,0:T(8,128)} %param.14) | copy-start | bytes 589828
Sparse Core Ops, SparseCore 0:
  24.7 42.3 all-gather.1
  144.8 19.6 reduce-scatter.4
  166.7 21.2 reduce-scatter.2
